TPU v7x, 32 devices: a whole 2x2x4 slice. The times are simulated.
32 devices in a mesh: mp: 2 (over core), feat: 16 (over z, y, x).
Axes of the slice: x: 2, y: 2, z: 4, core: 2. Of those that a mesh axis runs over, the one named last changes fastest.
Arguments:
- residual: bfloat16 [2, 96, 2304], P(None, 'feat', 'mp'), may hold values from -6 to 6
- norm_gain: float32 [2, 2304], P(None, 'mp'), may hold values from 0.1 to 1.9
- gate_weight: bfloat16 [2, 2304, 9216], P(None, 'mp', 'feat'), may hold values from -0.125 to 0.125
- up_weight: bfloat16 [2, 2304, 9216], P(None, 'mp', 'feat'), may hold values from -0.125 to 0.125
- down_weight: bfloat16 [2, 9216, 2304], P(None, 'feat', 'mp'), may hold values from -0.0625 to 0.0625
- encoder: bfloat16 [2, 32768, 2304], P(None, 'feat', 'mp'), may hold values from -0.125 to 0.125
- encoder_bias: float32 [2, 32768], P(None, 'feat'), may hold values from -3 to 3
- decoder: bfloat16 [3, 32768, 2304], P(None, 'feat', 'mp'), may hold values from -0.03125 to 0.03125
Outputs:
- grad_encoder: bfloat16 [2, 32768, 2304], P(None, 'feat', 'mp')
- grad_bias: float32 [2, 32768], P(None, 'feat')
- grad_decoder: bfloat16 [3, 32768, 2304], P(None, 'feat', 'mp')
All inputs are finite; a program needn't handle non-finite values.
Results may differ from a plain program's by a relative error of at most 0.02.
The roundings to bfloat16 on the way count: a program that leaves them out, or rounds other values in their place, can miss the bound.
Values may be sent and summed in bfloat16 or wider, within the bound.
No kernel may reach another device: no remote copies, remote signals or barrier semaphores. Data moves between devices by JAX's collectives and lax.ppermute only.
A program may use at most 128 MiB of HBM per device.

v0:
```python
import math
import jax
import jax.numpy as jnp
from jax import lax
from jax.sharding import PartitionSpec as P

D = 2304
sparsity_weight = 0.1


def outer_product(weights_side, errors_side):
    return lax.dot_general(
        weights_side, errors_side, (((0,), (0,)), ((), ())), preferred_element_type=jnp.float32
    )


def body(residual, norm_gain, gate_weight, up_weight, down_weight, encoder, encoder_bias, decoder):
    values = residual.astype(jnp.float32)
    squares = lax.psum(jnp.sum(values * values, axis=2), "mp")
    inverse_rms = lax.rsqrt(squares / D + 1e-06)
    normed_local = (values * inverse_rms[:, :, None] * norm_gain[:, None, :]).astype(jnp.bfloat16)
    normed = lax.all_gather(normed_local, "feat", axis=1, tiled=True)
    tokens = normed.shape[1]
    local_rows = residual.shape[1]
    gate_part = jnp.einsum("ltd,ldh->lth", normed, gate_weight, preferred_element_type=jnp.float32)
    up_part = jnp.einsum("ltd,ldh->lth", normed, up_weight, preferred_element_type=jnp.float32)
    gate_part, up_part = (
        lax.psum(gate_part.astype(jnp.bfloat16), "mp").astype(jnp.float32),
        lax.psum(up_part.astype(jnp.bfloat16), "mp").astype(jnp.float32),
    )
    hidden = (jax.nn.gelu(gate_part, approximate=True) * up_part).astype(jnp.bfloat16)
    preact_part = jnp.einsum("ltd,lfd->tlf", normed, encoder, preferred_element_type=jnp.float32)
    preact = lax.psum(preact_part, "mp")
    active = jnp.maximum(preact + encoder_bias[None], 0.0).astype(jnp.bfloat16)
    features = active.shape[2]
    model_cols = decoder.shape[2]
    joined = jnp.concatenate([decoder[1], decoder[2]], axis=0)
    picked = hidden
    partial_value = jnp.einsum(
        "lth,lhd->tld", picked, down_weight, preferred_element_type=jnp.float32
    )
    picked = active
    first_part = jnp.dot(picked[:, 0], decoder[0], preferred_element_type=jnp.float32)
    second = jnp.dot(
        picked.reshape(local_rows * lax.axis_size("feat"), 2 * features),
        joined,
        preferred_element_type=jnp.float32,
    )
    errors_local = lax.psum_scatter(
        jnp.concatenate([first_part, second], axis=1)
        - partial_value.reshape(local_rows * lax.axis_size("feat"), -1),
        "feat",
        scatter_dimension=0,
        tiled=True,
    ).astype(jnp.bfloat16)
    errors = lax.all_gather(errors_local, "feat", axis=0, tiled=True)
    error_first = errors[:, :model_cols]
    error_second = errors[:, model_cols:]
    first_rows = jnp.concatenate([decoder[0], decoder[1]], axis=1)
    back_first = lax.dot_general(
        errors, first_rows, (((1,), (1,)), ((), ())), preferred_element_type=jnp.float32
    )
    back_second = lax.dot_general(
        error_second, decoder[2], (((1,), (1,)), ((), ())), preferred_element_type=jnp.float32
    )
    back_stack = jnp.stack([back_first, back_second], axis=1)
    loss_scale = 1.0 / math.sqrt(tokens)
    backward = lax.psum(back_stack.astype(jnp.bfloat16), "mp").astype(jnp.float32)
    pre_grad = jnp.where(active > 0, loss_scale * (backward + sparsity_weight), 0.0).astype(
        jnp.bfloat16
    )
    grad_encoder = jnp.einsum(
        "tlf,ltd->lfd", pre_grad, normed, preferred_element_type=jnp.float32
    ).astype(jnp.bfloat16)
    grad_bias = jnp.sum(pre_grad.astype(jnp.float32), axis=0)
    active_first = active[:, 0]
    active_second = active[:, 1]
    grad_decoder = (
        loss_scale
        * jnp.stack(
            [
                outer_product(active_first, error_first),
                outer_product(active_first, error_second),
                outer_product(active_second, error_second),
            ]
        )
    ).astype(jnp.bfloat16)
    return (grad_encoder, grad_bias, grad_decoder)


def solution(mesh):
    return jax.shard_map(
        body,
        mesh=mesh,
        in_specs=(
            P(None, "feat", "mp"),
            P(None, "mp"),
            P(None, "mp", "feat"),
            P(None, "mp", "feat"),
            P(None, "feat", "mp"),
            P(None, "feat", "mp"),
            P(None, "feat"),
            P(None, "feat", "mp"),
        ),
        out_specs=(P(None, "feat", "mp"), P(None, "feat"), P(None, "feat", "mp")),
        check_vma=False,
    )
```

profile of v0, /device:TPU:0, one launch (start us, length us, event | category | flops | bytes accessed | tf_op | source)
XLA Modules:
  0.0 270.2 jit_solution(11253927287694514613)
XLA Ops:
  7.2 0.0 copy-start
  7.2 0.0 all-reduce.11.cloned.1.call-start
  7.2 1.0 fusion.38
  8.2 2.6 psum.35
  10.9 0.8 fusion.40
  11.7 44.8 %all_gather.6 = bf16[2,96,1152]{2,0,1:T(2,128)(2,1)S(1)} all-gather(bf16[2,6,1152]{2,0,1:T(2,128)(2,1)S(1)} %fusion.40), channel_id=1, replica_groups=mesh['mp'=2,'feat'=16] {'feat'}, dimensions={1}, use_global_device_ids=true | all-gather | bytes 470016 | tf_op jit(solution)/shard_map/all_gather | solution.py:22
  56.5 0.0 copy-start.3
  56.5 3.6 %convolution_convert_fusion.3 = bf16[2,96,576]{2,1,0:T(8,128)(2,1)} fusion(bf16[2,1152,576]{1,2,0:T(8,128)(2,1)} %param.10, bf16[2,96,1152]{2,0,1:T(2,128)(2,1)S(1)} %all_gather.6), kind=kOutput, calls=%fused_computation.27 | convolution fusion | flops 254914560 | bytes 3317760 | tf_op jit(solution)/shard_map/ltd,ldh->lth/dot_general | solution.py:25
  60.1 3.4 %convolution_convert_fusion.2 = bf16[2,96,576]{2,1,0:T(8,128)(2,1)} fusion(bf16[2,1152,576]{1,2,0:T(8,128)(2,1)} %param.11, bf16[2,96,1152]{2,0,1:T(2,128)(2,1)S(1)} %all_gather.6), kind=kOutput, calls=%fused_computation.26 | convolution fusion | flops 254914560 | bytes 3317760 | tf_op jit(solution)/shard_map/ltd,ldh->lth/dot_general | solution.py:26
  63.5 0.0 all-reduce.11.cloned.1.call-update
  63.5 0.0 all-reduce.7.cloned.1.call-start
  63.6 8.0 %convolution_bitcast_fusion.4 = f32[96,2,2048]{2,0,1:T(8,128)} fusion(bf16[2,2048,1152]{2,1,0:T(8,128)(2,1)} %param.13, bf16[2,96,1152]{2,0,1:T(2,128)(2,1)S(1)} %all_gather.6), kind=kOutput, calls=%fused_computation.18 | convolution fusion | flops 905969664 | bytes 11452416 | tf_op jit(solution)/shard_map/ltd,lfd->tlf/dot_general | solution.py:32
  71.6 0.0 copy-done.3
  71.6 0.0 all-reduce.7.cloned.1.call-update
  71.6 0.0 all-reduce.9.cloned.1.call-start
  71.7 11.3 %slice_bitcast_fusion.2 = (bf16[2048,1152]{1,0:T(8,128)(2,1)}, bf16[2048,1152]{1,0:T(8,128)(2,1)}, bf16[2048,1152]{1,0:T(8,128)(2,1)}) fusion(bf16[3,2048,1152]{2,1,0:T(8,128)(2,1)} %param.15), kind=kLoop, calls=%fused_computation.16 | loop fusion | bytes 28311552 | tf_op jit(solution)/shard_map/squeeze | solution.py:43
  83.0 0.0 copy-start.5
  83.0 0.0 all-reduce.11.cloned.1.call-done
  83.0 0.0 copy-done
  83.0 1.7 convolution_bitcast_fusion.3
  84.7 0.1 copy.23
  84.8 17.4 %all-reduce.7.cloned.1.call-done = f32[96,2,2048]{2,0,1:T(8,128)} async-done(((f32[96,2,2048]{2,0,1:T(8,128)}), f32[96,2,2048]{2,0,1:T(8,128)}) %all-reduce.7.cloned.1.call-update) | async-done | bytes 1572880 | tf_op jit(solution)/shard_map/psum | solution.py:33
  102.1 0.0 copy-done.5
  102.1 1.7 maximum_convert_fusion
  103.9 0.0 slice-start.3
  103.9 0.0 copy-start.4
  103.9 3.7 %fusion.24 = f32[96,1152]{1,0:T(8,128)S(1)} fusion(bf16[96,2,2048]{2,0,1:T(8,128)(2,1)S(1)} %maximum_convert_fusion, bf16[3,2048,1152]{2,1,0:T(8,128)(2,1)} %param.15), kind=kOutput, calls=%fused_computation.43 | convolution fusion | flops 452984832 | bytes 5554176 | tf_op jit(solution)/shard_map/dot_general | solution.py:43
  107.6 0.0 copy-done.2
  107.6 0.2 fusion.59
  107.8 0.1 copy.22
  107.8 0.0 slice-done.2
  107.8 0.0 slice-done.3
  107.9 0.6 copy-done.4
  108.5 2.0 fusion.2
  110.5 0.1 maximum_subtract_fusion
  110.6 49.0 %fusion = f32[8,2304]{1,0:T(8,128)S(1)} fusion(f32[96,2304]{1,0:T(8,128)S(1)} %maximum_subtract_fusion), kind=kCustom, calls=%all-reduce-scatter | all-reduce-scatter fusion | flops 294913 | bytes 958976
  159.6 1.3 collective-permute-start.1
  160.9 1.3 collective-permute-start.2
  162.2 1.9 collective-permute-start
  164.1 2.4 collective-permute-start.3
  166.5 0.0 copy-done.6
  166.5 0.6 dynamic-slice.4
  167.8 0.4 collective-permute-done.3
  168.1 0.0 collective-permute-done.1
  168.1 0.0 collective-permute-done.2
  168.1 0.0 collective-permute-done
  168.1 0.6 concatenate.12
  168.8 43.6 %all-gather = bf16[16,6,2304]{2,1,0:T(8,128)(2,1)S(1)} all-gather(bf16[1,6,2304]{2,1,0:T(8,128)(2,1)S(1)} %fusion.41), channel_id=1, replica_groups=mesh['mp'=2,'feat'=16] {'feat'}, dimensions={0}, use_global_device_ids=true | all-gather | bytes 470016 | tf_op jit(solution)/shard_map/all_gather | solution.py:56
  212.4 0.1 reshape.18
  212.5 3.9 %fusion.16 = bf16[96,1,2048]{2,0,1:T(8,128)(2,1)S(1)} fusion(bf16[96,2304]{1,0:T(8,128)(2,1)S(1)} %reshape.18, bf16[3,2048,1152]{2,1,0:T(8,128)(2,1)} %param.15), kind=kOutput, calls=%fused_computation.22 | convolution fusion | flops 453181440 | bytes 5332992 | tf_op jit(solution)/shard_map/dot_general | solution.py:63
  216.4 5.1 %convolution_bitcast_fusion.1 = f32[1,2048,1152]{2,1,0:T(8,128)} fusion(bf16[96,2,2048]{2,0,1:T(8,128)(2,1)S(1)} %maximum_convert_fusion, bf16[96,2304]{1,0:T(8,128)(2,1)S(1)} %reshape.18), kind=kOutput, calls=%fused_computation.12 | convolution fusion | flops 452984832 | bytes 10051584 | tf_op jit(solution)/shard_map/dot_general | solution.py:12
  221.5 5.8 %convolution_bitcast_fusion = f32[1,2048,1152]{2,1,0:T(8,128)} fusion(bf16[96,2,2048]{2,0,1:T(8,128)(2,1)S(1)} %maximum_convert_fusion, bf16[96,2304]{1,0:T(8,128)(2,1)S(1)} %reshape.18), kind=kOutput, calls=%fused_computation.11 | convolution fusion | flops 452984832 | bytes 10051584 | tf_op jit(solution)/shard_map/dot_general | solution.py:12
  227.3 5.1 %convolution_bitcast_fusion.2 = f32[1,2048,1152]{2,1,0:T(8,128)} fusion(bf16[96,2,2048]{2,0,1:T(8,128)(2,1)S(1)} %maximum_convert_fusion, bf16[96,2304]{1,0:T(8,128)(2,1)S(1)} %reshape.18), kind=kOutput, calls=%fused_computation.13 | convolution fusion | flops 452984832 | bytes 10051584 | tf_op jit(solution)/shard_map/dot_general | solution.py:12
  232.4 0.0 slice-done
  232.4 0.0 slice-done.4
  232.4 0.0 slice-done.1
  232.4 0.0 slice-done.5
  232.4 3.1 %fusion.13 = bf16[96,1,2048]{2,0,1:T(8,128)(2,1)S(1)} fusion(bf16[96,2304]{1,0:T(8,128)(2,1)S(1)} %reshape.18, bf16[2048,1152]{1,0:T(8,128)(2,1)S(1)} %bitcast.51, bf16[2048,1152]{1,0:T(8,128)(2,1)S(1)} %bitcast.47), kind=kOutput, calls=%fused_computation.21 | convolution fusion | flops 925040640 | bytes 10272768 | tf_op jit(solution)/shard_map/dot_general | solution.py:60
  235.6 1.0 pad_maximum_fusion
  236.5 0.0 all-reduce.9.cloned.1.call-update
  236.5 16.6 %fusion.1 = bf16[3,2048,1152]{2,1,0:T(8,128)(2,1)} fusion(f32[1,2048,1152]{2,1,0:T(8,128)} %convolution_bitcast_fusion, f32[1,2048,1152]{2,1,0:T(8,128)} %convolution_bitcast_fusion.1, f32[1,2048,1152]{2,1,0:T(8,128)} %convolution_bitcast_fusion.2), kind=kLoop, calls=%fused_computation.1 | loop fusion | flops 28311552 | bytes 42467328 | tf_op jit(solution)/shard_map/convert_element_type | solution.py:87
  253.2 2.8 %convert_reduce_fusion = f32[2,2048]{1,0:T(2,128)} fusion(bf16[96,2,2048]{2,0,1:T(8,128)(2,1)} %all-reduce.9.cloned.1.call-done, f32[96,2,2048]{2,0,1:T(8,128)} %all-reduce.7.cloned.1.call-done, f32[2,2048]{1,0:T(2,128)S(1)} %copy-done.5), kind=kLoop, calls=%fused_computation.23 | loop fusion | flops 4321280 | bytes 2392064 | tf_op jit(solution)/shard_map/reduce_sum | solution.py:75
  256.0 7.6 %convolution_convert_fusion = bf16[2,2048,1152]{2,1,0:T(8,128)(2,1)} fusion(bf16[2,96,1152]{2,0,1:T(2,128)(2,1)} %copy-done.3, bf16[96,2,2048]{2,0,1:T(8,128)(2,1)} %all-reduce.9.cloned.1.call-done, bf16[96,2,2048]{2,0,1:T(8,128)(2,1)S(1)} %maximum_convert_fusion), kind=kOutput, calls=%fused_computation.2 | convolution fusion | flops 913047552 | bytes 11452416 | tf_op jit(solution)/shard_map/tlf,ltd->lfd/dot_general | solution.py:72
  263.7 0.0 copy-done.1
  (16 shorter events, 0.1 us)
Async XLA Ops:
  7.2 75.8 %copy-start = (bf16[2,576,1152]{2,1,0:T(8,128)(2,1)S(1)}, bf16[2,576,1152]{2,1,0:T(8,128)(2,1)}, u32[]{:S(2)}) copy-start(bf16[2,576,1152]{2,1,0:T(8,128)(2,1)} %param.12) | copy-start | bytes 7962628
  7.2 75.8 %all-reduce.11.cloned.1.call-start = ((), (), s32[]{:S(2)}) async-start(), calls=%async_computation.2 | async-start | bytes 983040 | tf_op jit(solution)/shard_map/psum | solution.py:28
  56.5 15.0 %copy-start.3 = (bf16[2,96,1152]{2,0,1:T(2,128)(2,1)}, bf16[2,96,1152]{2,0,1:T(2,128)(2,1)S(1)}, u32[]{:S(2)}) copy-start(bf16[2,96,1152]{2,0,1:T(2,128)(2,1)S(1)} %all_gather.6) | copy-start | bytes 1327108
  63.5 38.6 %all-reduce.7.cloned.1.call-start = ((), (), s32[]{:S(2)}) async-start(), calls=%async_computation | async-start | bytes 3145728 | tf_op jit(solution)/shard_map/psum | solution.py:33
  71.6 181.6 %all-reduce.9.cloned.1.call-start = ((), (), s32[]{:S(2)}) async-start(), calls=%async_computation.1 | async-start | bytes 1572864 | tf_op jit(solution)/shard_map/psum | solution.py:68
  83.0 19.1 %copy-start.5 = (f32[2,2048]{1,0:T(2,128)S(1)}, f32[2,2048]{1,0:T(2,128)}, u32[]{:S(2)}) copy-start(f32[2,2048]{1,0:T(2,128)} %param.14) | copy-start | bytes 49156
  102.1 5.4 %copy-start.2 = (f32[96,2,2048]{2,0,1:T(8,128)S(1)}, f32[96,2,2048]{2,0,1:T(8,128)}, u32[]{:S(2)}) copy-start(f32[96,2,2048]{2,0,1:T(8,128)} %all-reduce.7.cloned.1.call-done) | copy-start | bytes 4718596
  102.1 5.7 %slice-start.2 = ((s8[4718592]{0:T(1024)(128)(4,1)}), s8[4194304]{0:T(1024)(128)(4,1)S(1)}, s32[]{:S(2)}) async-start(s8[4718592]{0:T(1024)(128)(4,1)} %bitcast.48), calls=%async_computation.5 | async-start | bytes 8388608
  103.9 4.0 %slice-start.3 = ((s8[4718592]{0:T(1024)(128)(4,1)}), s8[524288]{0:T(1024)(128)(4,1)S(1)}, s32[]{:S(2)}) async-start(s8[4718592]{0:T(1024)(128)(4,1)} %bitcast.48), calls=%async_computation.6 | async-start | bytes 1048576
  103.9 4.6 %copy-start.4 = (bf16[2048,1152]{1,0:T(8,128)(2,1)S(1)}, bf16[2048,1152]{1,0:T(8,128)(2,1)}, u32[]{:S(2)}) copy-start(bf16[2048,1152]{1,0:T(8,128)(2,1)} %get-tuple-element.6) | copy-start | bytes 14155780
  108.5 58.1 %copy-start.6 = (u32[32]{0:T(128)S(1)}, u32[32]{0:T(128)}, u32[]{:S(2)}) copy-start(u32[32]{0:T(128)} %constant.26) | copy-start | bytes 388
  159.6 8.5 %collective-permute-start.1 = (bf16[8,2304]{1,0:T(8,128)(2,1)S(1)}, bf16[8,2304]{1,0:T(8,128)(2,1)S(1)}, u32[]{:S(2)}, u32[]{:S(2)}) collective-permute-start(bf16[8,2304]{1,0:T(8,128)(2,1)S(1)} %convert.22), channel_id=1, source_target_pairs={{0,2},{1,3},{2,4},{3,5},{4,6},{5,7},{6,8},{7,9},{8,10},{9,11},{10,... | collective-permute-start | bytes 110600
  160.9 7.2 %collective-permute-start.2 = (bf16[8,2304]{1,0:T(8,128)(2,1)S(1)}, bf16[8,2304]{1,0:T(8,128)(2,1)S(1)}, u32[]{:S(2)}, u32[]{:S(2)}) collective-permute-start(bf16[8,2304]{1,0:T(8,128)(2,1)S(1)} %convert.22), channel_id=1, source_target_pairs={{0,3},{1,4},{2,5},{3,6},{4,7},{5,8},{6,9},{7,10},{8,11},{9,12},{10... | collective-permute-start | bytes 110600
  162.2 5.9 %collective-permute-start = (bf16[8,2304]{1,0:T(8,128)(2,1)S(1)}, bf16[8,2304]{1,0:T(8,128)(2,1)S(1)}, u32[]{:S(2)}, u32[]{:S(2)}) collective-permute-start(bf16[8,2304]{1,0:T(8,128)(2,1)S(1)} %convert.22), channel_id=1, source_target_pairs={{0,1},{1,2},{2,3},{3,4},{4,5},{5,6},{6,7},{7,8},{8,9},{9,10},{10,1... | collective-permute-start | bytes 110600
  164.1 4.0 %collective-permute-start.3 = (bf16[6,2304]{1,0:T(8,128)(2,1)S(1)}, bf16[6,2304]{1,0:T(8,128)(2,1)S(1)}, u32[]{:S(2)}, u32[]{:S(2)}) collective-permute-start(bf16[6,2304]{1,0:T(8,128)(2,1)S(1)} %slice.36), channel_id=1, source_target_pairs={{0,4},{1,5},{2,6},{3,7},{4,8},{5,9},{6,10},{7,11},{8,12},{9,13},{1... | collective-permute-start | bytes 82952
  221.5 10.9 %slice-start = ((s8[4718592]{0:T(1024)(128)(4,1)}), s8[4194304]{0:T(1024)(128)(4,1)S(1)}, s32[]{:S(2)}) async-start(s8[4718592]{0:T(1024)(128)(4,1)} %bitcast.46), calls=%async_computation.3 | async-start | bytes 8388608
  221.5 10.9 %slice-start.4 = ((s8[4718592]{0:T(1024)(128)(4,1)}), s8[4194304]{0:T(1024)(128)(4,1)S(1)}, s32[]{:S(2)}) async-start(s8[4718592]{0:T(1024)(128)(4,1)} %bitcast.50), calls=%async_computation.7 | async-start | bytes 8388608
  227.3 5.1 %slice-start.1 = ((s8[4718592]{0:T(1024)(128)(4,1)}), s8[524288]{0:T(1024)(128)(4,1)S(1)}, s32[]{:S(2)}) async-start(s8[4718592]{0:T(1024)(128)(4,1)} %bitcast.46), calls=%async_computation.4 | async-start | bytes 1048576
  227.3 5.1 %slice-start.5 = ((s8[4718592]{0:T(1024)(128)(4,1)}), s8[524288]{0:T(1024)(128)(4,1)S(1)}, s32[]{:S(2)}) async-start(s8[4718592]{0:T(1024)(128)(4,1)} %bitcast.50), calls=%async_computation.8 | async-start | bytes 1048576
  253.2 10.5 %copy-start.1 = (bf16[2,576,1152]{2,1,0:T(8,128)(2,1)S(1)}, bf16[2,576,1152]{2,1,0:T(8,128)(2,1)}, u32[]{:S(2)}) copy-start(bf16[2,576,1152]{2,1,0:T(8,128)(2,1)} %param.12) | copy-start | bytes 7962628
Sparse Core Ops, SparseCore 0:
  63.6 14.4 all-reduce.10
  80.5 21.5 all-reduce.6
  236.7 14.8 all-reduce.8
where the time goes:
time: 271 us; the launch traced here: 270 us
  blocking collectives  140 us (52%)
  matrix products  53 us (20%)
  other arithmetic  24.3 us (9%)
  waiting for transfers between devices  17.8 us (7%)
  between operations  14.6 us (5%)
  local copies, waits for them, and re-layouts  13.5 us (5%)
  starting transfers between devices  6.99 us (3%)
    unnamed x1, blocking collectives  49 us
    all_gather x1, blocking collectives, body(): normed = lax.all_gather(normed_local, 'feat', axis=1, tiled=True)  44.8 us
    all_gather x1, blocking collectives, body(): errors = lax.all_gather(errors_local, 'feat', axis=0, tiled=True)  43.6 us
    psum x1, waiting for transfers between devices, body(): preact = lax.psum(preact_part, 'mp')  17.4 us
    convert_element_type x1, other arithmetic, body(): grad_decoder = (loss_scale * jnp.stack([outer_product(active_first, error...  16.6 us
    dot_general x3, matrix products, outer_product(): lax.dot_general(weights_side, errors_side, (((0,), (0,)), ((), ())), pref...  15.9 us
    squeeze x1, local copies, waits for them, and re-layouts, body(): decoder[0]  11.3 us
    dot_general x1, matrix products, body(): jnp.einsum('ltd,lfd->tlf', normed, encoder, preferred_element_type=jnp.fl...  8.01 us
  transfers between devices with their start and end apart: 7, of which 2 were waited for; matrix products, arithmetic and copies ran while one was open for 14% of the time, Pallas kernels for 0%

commit v1 on v0

--- a/solution.py
+++ b/solution.py
@@ -19,7 +19,12 @@
     squares = lax.psum(jnp.sum(values * values, axis=2), "mp")
     inverse_rms = lax.rsqrt(squares / D + 1e-06)
     normed_local = (values * inverse_rms[:, :, None] * norm_gain[:, None, :]).astype(jnp.bfloat16)
-    normed = lax.all_gather(normed_local, "feat", axis=1, tiled=True)
+    ring = [normed_local]
+    for hop in range(15):
+        ring.append(lax.ppermute(ring[-1], "feat", [(dev, (dev + 1) % 16) for dev in range(16)]))
+    normed = jnp.roll(
+        jnp.concatenate(ring[::-1], axis=1), (lax.axis_index("feat") + 1) * ring[0].shape[1], axis=1
+    )
     tokens = normed.shape[1]
     local_rows = residual.shape[1]
     gate_part = jnp.einsum("ltd,ldh->lth", normed, gate_weight, preferred_element_type=jnp.float32)

time: 271 us -> 379 us (1.40)
  waiting for transfers between devices: 17.8 us -> 129 us
  blocking collectives: 140 us -> 95.2 us
  local copies, waits for them, and re-layouts: 13.5 us -> 49.9 us
    ppermute x0 -> x15, waiting for transfers between devices: none -> 111 us  [body(): lax.ppermute(ring[-1], 'feat', [(dev, (dev + 1) % 16) for dev in range(16)])]
    all_gather x1 -> x0, blocking collectives: 44.8 us -> none  [body(): normed = lax.all_gather(normed_local, 'feat', axis=1, tiled=True)]
    concatenate x0 -> x1, local copies, waits for them, and re-layouts: none -> 27.4 us  [body(): jnp.roll(jnp.concatenate(ring[::-1], axis=1), (lax.axis_index('feat') + 1...]
    unnamed x31 -> x61, local copies, waits for them, and re-layouts: 2.02 us -> 11.2 us
  transfers between devices with their start and end apart: 7 -> 22, of which waited for: 2 -> 17; matrix products, arithmetic and copies ran while one was open for 14% -> 10% of each run, Pallas kernels for 0% -> 0%
where the time goes in v1:
time: 379 us; the launch traced here: 376 us
  waiting for transfers between devices  129 us (34%)
  blocking collectives  95.2 us (25%)
  matrix products  53.3 us (14%)
  local copies, waits for them, and re-layouts  49.9 us (13%)
  other arithmetic  24.3 us (6%)
  between operations  14.7 us (4%)
  starting transfers between devices  9.83 us (3%)
    ppermute x15, waiting for transfers between devices, body(): lax.ppermute(ring[-1], 'feat', [(dev, (dev + 1) % 16) for dev in range(16)])  111 us
    unnamed x1, blocking collectives  49 us
    all_gather x1, blocking collectives, body(): errors = lax.all_gather(errors_local, 'feat', axis=0, tiled=True)  43.6 us
    concatenate x1, local copies, waits for them, and re-layouts, body(): jnp.roll(jnp.concatenate(ring[::-1], axis=1), (lax.axis_index('feat') + 1...  27.4 us
    psum x1, waiting for transfers between devices, body(): preact = lax.psum(preact_part, 'mp')  17.3 us
    convert_element_type x1, other arithmetic, body(): grad_decoder = (loss_scale * jnp.stack([outer_product(active_first, error...  16.6 us
    dot_general x3, matrix products, outer_product(): lax.dot_general(weights_side, errors_side, (((0,), (0,)), ((), ())), pref...  15.9 us
    squeeze x1, local copies, waits for them, and re-layouts, body(): decoder[0]  11.3 us
  transfers between devices with their start and end apart: 22, of which 17 were waited for; matrix products, arithmetic and copies ran while one was open for 10% of the time, Pallas kernels for 0%

profile of v1, /device:TPU:0, one launch (start us, length us, event | category | flops | bytes accessed | tf_op | source)
XLA Modules:
  0.0 376.1 jit_solution(5873283820091917898)
XLA Ops:
  7.2 1.0 fusion.38
  8.2 2.6 psum.35
  10.8 0.8 fusion.40
  11.7 0.6 copy-done.5
  12.3 2.8 collective-permute-start
  15.1 5.9 %collective-permute-done = bf16[2,6,1152]{2,1,0:T(8,128)(2,1)S(1)} collective-permute-done((bf16[2,6,1152]{2,1,0:T(8,128)(2,1)S(1)}, bf16[2,6,1152]{2,1,0:T(8,128)(2,1)S(1)}, u32[]{:S(2)}, u32[]{:S(2)}) %collective-permute-start) | collective-permute-done | bytes 27680 | tf_op jit(solution)/shard_map/ppermute | solution.py:24
  21.0 0.6 copy-done.7
  21.6 7.6 %collective-permute-done.1 = bf16[2,6,1152]{2,1,0:T(8,128)(2,1)S(1)} collective-permute-done((bf16[2,6,1152]{2,1,0:T(8,128)(2,1)S(1)}, bf16[2,6,1152]{2,1,0:T(8,128)(2,1)S(1)}, u32[]{:S(2)}, u32[]{:S(2)}) %collective-permute-start.1) | collective-permute-done | bytes 27680 | tf_op jit(solution)/shard_map/ppermute | solution.py:24
  29.2 0.6 copy-done.8
  29.8 7.6 %collective-permute-done.2 = bf16[2,6,1152]{2,1,0:T(8,128)(2,1)S(1)} collective-permute-done((bf16[2,6,1152]{2,1,0:T(8,128)(2,1)S(1)}, bf16[2,6,1152]{2,1,0:T(8,128)(2,1)S(1)}, u32[]{:S(2)}, u32[]{:S(2)}) %collective-permute-start.2) | collective-permute-done | bytes 27680 | tf_op jit(solution)/shard_map/ppermute | solution.py:24
  37.4 0.6 copy-done.9
  38.0 7.6 %collective-permute-done.3 = bf16[2,6,1152]{2,1,0:T(8,128)(2,1)S(1)} collective-permute-done((bf16[2,6,1152]{2,1,0:T(8,128)(2,1)S(1)}, bf16[2,6,1152]{2,1,0:T(8,128)(2,1)S(1)}, u32[]{:S(2)}, u32[]{:S(2)}) %collective-permute-start.3) | collective-permute-done | bytes 27680 | tf_op jit(solution)/shard_map/ppermute | solution.py:24
  45.5 0.6 copy-done.10
  46.1 7.6 %collective-permute-done.4 = bf16[2,6,1152]{2,1,0:T(8,128)(2,1)S(1)} collective-permute-done((bf16[2,6,1152]{2,1,0:T(8,128)(2,1)S(1)}, bf16[2,6,1152]{2,1,0:T(8,128)(2,1)S(1)}, u32[]{:S(2)}, u32[]{:S(2)}) %collective-permute-start.4) | collective-permute-done | bytes 27680 | tf_op jit(solution)/shard_map/ppermute | solution.py:24
  53.7 0.6 copy-done.11
  54.3 7.6 %collective-permute-done.5 = bf16[2,6,1152]{2,1,0:T(8,128)(2,1)S(1)} collective-permute-done((bf16[2,6,1152]{2,1,0:T(8,128)(2,1)S(1)}, bf16[2,6,1152]{2,1,0:T(8,128)(2,1)S(1)}, u32[]{:S(2)}, u32[]{:S(2)}) %collective-permute-start.5) | collective-permute-done | bytes 27680 | tf_op jit(solution)/shard_map/ppermute | solution.py:24
  61.8 0.6 copy-done.12
  62.5 7.6 %collective-permute-done.6 = bf16[2,6,1152]{2,1,0:T(8,128)(2,1)S(1)} collective-permute-done((bf16[2,6,1152]{2,1,0:T(8,128)(2,1)S(1)}, bf16[2,6,1152]{2,1,0:T(8,128)(2,1)S(1)}, u32[]{:S(2)}, u32[]{:S(2)}) %collective-permute-start.6) | collective-permute-done | bytes 27680 | tf_op jit(solution)/shard_map/ppermute | solution.py:24
  70.0 0.6 copy-done.13
  70.6 7.6 %collective-permute-done.7 = bf16[2,6,1152]{2,1,0:T(8,128)(2,1)S(1)} collective-permute-done((bf16[2,6,1152]{2,1,0:T(8,128)(2,1)S(1)}, bf16[2,6,1152]{2,1,0:T(8,128)(2,1)S(1)}, u32[]{:S(2)}, u32[]{:S(2)}) %collective-permute-start.7) | collective-permute-done | bytes 27680 | tf_op jit(solution)/shard_map/ppermute | solution.py:24
  78.2 0.6 copy-done.14
  78.8 7.6 %collective-permute-done.8 = bf16[2,6,1152]{2,1,0:T(8,128)(2,1)S(1)} collective-permute-done((bf16[2,6,1152]{2,1,0:T(8,128)(2,1)S(1)}, bf16[2,6,1152]{2,1,0:T(8,128)(2,1)S(1)}, u32[]{:S(2)}, u32[]{:S(2)}) %collective-permute-start.8) | collective-permute-done | bytes 27680 | tf_op jit(solution)/shard_map/ppermute | solution.py:24
  86.3 0.6 copy-done.15
  87.0 7.6 %collective-permute-done.9 = bf16[2,6,1152]{2,1,0:T(8,128)(2,1)S(1)} collective-permute-done((bf16[2,6,1152]{2,1,0:T(8,128)(2,1)S(1)}, bf16[2,6,1152]{2,1,0:T(8,128)(2,1)S(1)}, u32[]{:S(2)}, u32[]{:S(2)}) %collective-permute-start.9) | collective-permute-done | bytes 27680 | tf_op jit(solution)/shard_map/ppermute | solution.py:24
  94.5 0.6 copy-done.16
  95.1 7.6 %collective-permute-done.10 = bf16[2,6,1152]{2,1,0:T(8,128)(2,1)S(1)} collective-permute-done((bf16[2,6,1152]{2,1,0:T(8,128)(2,1)S(1)}, bf16[2,6,1152]{2,1,0:T(8,128)(2,1)S(1)}, u32[]{:S(2)}, u32[]{:S(2)}) %collective-permute-start.10) | collective-permute-done | bytes 27680 | tf_op jit(solution)/shard_map/ppermute | solution.py:24
  102.7 0.6 copy-done.17
  103.3 7.6 %collective-permute-done.11 = bf16[2,6,1152]{2,1,0:T(8,128)(2,1)S(1)} collective-permute-done((bf16[2,6,1152]{2,1,0:T(8,128)(2,1)S(1)}, bf16[2,6,1152]{2,1,0:T(8,128)(2,1)S(1)}, u32[]{:S(2)}, u32[]{:S(2)}) %collective-permute-start.11) | collective-permute-done | bytes 27680 | tf_op jit(solution)/shard_map/ppermute | solution.py:24
  110.8 0.6 copy-done.18
  111.4 7.6 %collective-permute-done.12 = bf16[2,6,1152]{2,1,0:T(8,128)(2,1)S(1)} collective-permute-done((bf16[2,6,1152]{2,1,0:T(8,128)(2,1)S(1)}, bf16[2,6,1152]{2,1,0:T(8,128)(2,1)S(1)}, u32[]{:S(2)}, u32[]{:S(2)}) %collective-permute-start.12) | collective-permute-done | bytes 27680 | tf_op jit(solution)/shard_map/ppermute | solution.py:24
  119.0 0.6 copy-done.19
  119.6 7.6 %collective-permute-done.13 = bf16[2,6,1152]{2,1,0:T(8,128)(2,1)S(1)} collective-permute-done((bf16[2,6,1152]{2,1,0:T(8,128)(2,1)S(1)}, bf16[2,6,1152]{2,1,0:T(8,128)(2,1)S(1)}, u32[]{:S(2)}, u32[]{:S(2)}) %collective-permute-start.13) | collective-permute-done | bytes 27680 | tf_op jit(solution)/shard_map/ppermute | solution.py:24
  127.2 0.6 copy-done.20
  127.8 7.0 %collective-permute-done.14 = bf16[2,6,1152]{2,1,0:T(8,128)(2,1)} collective-permute-done((bf16[2,6,1152]{2,1,0:T(8,128)(2,1)S(1)}, bf16[2,6,1152]{2,1,0:T(8,128)(2,1)}, u32[]{:S(2)}, u32[]{:S(2)}) %collective-permute-start.14) | collective-permute-done | bytes 27680 | tf_op jit(solution)/shard_map/ppermute | solution.py:24
  134.8 27.4 %concatenate.15 = bf16[2,192,1152]{2,1,0:T(8,128)(2,1)S(1)} concatenate(bf16[2,6,1152]{2,1,0:T(8,128)(2,1)} %collective-permute-done.14, bf16[2,6,1152]{2,1,0:T(8,128)(2,1)} %copy-done.20, bf16[2,6,1152]{2,1,0:T(8,128)(2,1)} %copy-done.19, bf16[2,6,1152]{2,1,0:T(8,128)(2,1)} %copy-done.18, bf16[2,6,1152]{2,1,0:T(8,128)(2,1)} %copy-done.17, bf16[2,6,1152]{2,1,0:T(8,128)(2,1)} %copy-done.16, ...), dimensions={1} | concatenate | bytes 1769472 | tf_op jit(solution)/shard_map/jit(_roll_dynamic)/concatenate | solution.py:25
  162.2 3.8 convolution_convert_fusion.3
  165.9 3.4 convolution_convert_fusion.2
  169.4 8.0 %convolution_bitcast_fusion.4 = f32[96,2,2048]{2,0,1:T(8,128)} fusion(bf16[2,2048,1152]{2,1,0:T(8,128)(2,1)} %param.13, bf16[2,192,1152]{2,1,0:T(8,128)(2,1)S(1)} %concatenate.15, s32[]{:T(128)S(6)} %select_n.18), kind=kOutput, calls=%fused_computation.18 | convolution fusion | flops 905969664 | bytes 11452420 | tf_op jit(solution)/shard_map/ltd,lfd->tlf/dot_general | solution.py:37
  177.6 11.3 %slice_bitcast_fusion.2 = (bf16[2048,1152]{1,0:T(8,128)(2,1)}, bf16[2048,1152]{1,0:T(8,128)(2,1)}, bf16[2048,1152]{1,0:T(8,128)(2,1)}) fusion(bf16[3,2048,1152]{2,1,0:T(8,128)(2,1)} %param.15), kind=kLoop, calls=%fused_computation.16 | loop fusion | bytes 28311552 | tf_op jit(solution)/shard_map/squeeze | solution.py:48
  188.9 1.7 convolution_bitcast_fusion.3
  190.6 17.3 %all-reduce.7.cloned.1.call-done = f32[96,2,2048]{2,0,1:T(8,128)} async-done(((f32[96,2,2048]{2,0,1:T(8,128)}), f32[96,2,2048]{2,0,1:T(8,128)}) %all-reduce.7.cloned.1.call-update) | async-done | bytes 1572880 | tf_op jit(solution)/shard_map/psum | solution.py:38
  208.0 1.7 maximum_convert_fusion
  209.7 3.7 fusion.24
  213.4 0.2 fusion.63
  213.7 0.6 copy-done.4
  214.3 2.0 fusion.2
  216.5 49.0 %fusion = f32[8,2304]{1,0:T(8,128)S(1)} fusion(f32[96,2304]{1,0:T(8,128)S(1)} %maximum_subtract_fusion), kind=kCustom, calls=%all-reduce-scatter | all-reduce-scatter fusion | flops 294913 | bytes 958976
  265.5 1.3 collective-permute-start.16
  266.8 1.3 collective-permute-start.17
  268.1 1.9 collective-permute-start.15
  270.0 2.4 collective-permute-start.18
  272.4 0.6 dynamic-slice.4
  273.6 0.4 collective-permute-done.18
  274.0 0.6 concatenate.19
  274.6 43.6 %all-gather = bf16[16,6,2304]{2,1,0:T(8,128)(2,1)S(1)} all-gather(bf16[1,6,2304]{2,1,0:T(8,128)(2,1)S(1)} %fusion.41), channel_id=1, replica_groups=mesh['mp'=2,'feat'=16] {'feat'}, dimensions={0}, use_global_device_ids=true | all-gather | bytes 470016 | tf_op jit(solution)/shard_map/all_gather | solution.py:61
  318.4 3.9 %fusion.16 = bf16[96,1,2048]{2,0,1:T(8,128)(2,1)S(1)} fusion(bf16[96,2304]{1,0:T(8,128)(2,1)S(1)} %reshape.18, bf16[3,2048,1152]{2,1,0:T(8,128)(2,1)} %param.15), kind=kOutput, calls=%fused_computation.22 | convolution fusion | flops 453181440 | bytes 5332992 | tf_op jit(solution)/shard_map/dot_general | solution.py:68
  322.3 5.1 %convolution_bitcast_fusion.1 = f32[1,2048,1152]{2,1,0:T(8,128)} fusion(bf16[96,2,2048]{2,0,1:T(8,128)(2,1)S(1)} %maximum_convert_fusion, bf16[96,2304]{1,0:T(8,128)(2,1)S(1)} %reshape.18), kind=kOutput, calls=%fused_computation.12 | convolution fusion | flops 452984832 | bytes 10051584 | tf_op jit(solution)/shard_map/dot_general | solution.py:12
  327.4 5.8 %convolution_bitcast_fusion = f32[1,2048,1152]{2,1,0:T(8,128)} fusion(bf16[96,2,2048]{2,0,1:T(8,128)(2,1)S(1)} %maximum_convert_fusion, bf16[96,2304]{1,0:T(8,128)(2,1)S(1)} %reshape.18), kind=kOutput, calls=%fused_computation.11 | convolution fusion | flops 452984832 | bytes 10051584 | tf_op jit(solution)/shard_map/dot_general | solution.py:12
  333.2 5.1 %convolution_bitcast_fusion.2 = f32[1,2048,1152]{2,1,0:T(8,128)} fusion(bf16[96,2,2048]{2,0,1:T(8,128)(2,1)S(1)} %maximum_convert_fusion, bf16[96,2304]{1,0:T(8,128)(2,1)S(1)} %reshape.18), kind=kOutput, calls=%fused_computation.13 | convolution fusion | flops 452984832 | bytes 10051584 | tf_op jit(solution)/shard_map/dot_general | solution.py:12
  338.3 3.1 fusion.13
  341.4 1.0 pad_maximum_fusion
  342.4 16.6 %fusion.1 = bf16[3,2048,1152]{2,1,0:T(8,128)(2,1)} fusion(f32[1,2048,1152]{2,1,0:T(8,128)} %convolution_bitcast_fusion, f32[1,2048,1152]{2,1,0:T(8,128)} %convolution_bitcast_fusion.1, f32[1,2048,1152]{2,1,0:T(8,128)} %convolution_bitcast_fusion.2), kind=kLoop, calls=%fused_computation.1 | loop fusion | flops 28311552 | bytes 42467328 | tf_op jit(solution)/shard_map/convert_element_type | solution.py:92
  359.1 2.8 convert_reduce_fusion
  361.9 7.7 %convolution_convert_fusion = bf16[2,2048,1152]{2,1,0:T(8,128)(2,1)} fusion(bf16[2,192,1152]{2,1,0:T(8,128)(2,1)} %copy-done.3, s32[]{:T(128)S(6)} %select_n.18, bf16[96,2,2048]{2,0,1:T(8,128)(2,1)} %all-reduce.9.cloned.1.call-done, bf16[96,2,2048]{2,0,1:T(8,128)(2,1)S(1)} %maximum_convert_fusion), kind=kOutput, calls=%fused_computation.2 | convolution fusion | flops 913047552 | bytes 11452420 | tf_op jit(solution)/shard_map/tlf,ltd->lfd/dot_general | solution.py:77
  (76 shorter events, 0.7 us)
Async XLA Ops:
  7.2 181.7 %copy-start = (bf16[2,576,1152]{2,1,0:T(8,128)(2,1)S(1)}, bf16[2,576,1152]{2,1,0:T(8,128)(2,1)}, u32[]{:S(2)}) copy-start(bf16[2,576,1152]{2,1,0:T(8,128)(2,1)} %param.12) | copy-start | bytes 7962628
  7.2 181.7 %all-reduce.11.cloned.1.call-start = ((), (), s32[]{:S(2)}) async-start(), calls=%async_computation.2 | async-start | bytes 983040 | tf_op jit(solution)/shard_map/psum | solution.py:33
  11.7 0.6 copy-start.5
  12.3 8.7 %collective-permute-start = (bf16[2,6,1152]{2,1,0:T(8,128)(2,1)S(1)}, bf16[2,6,1152]{2,1,0:T(8,128)(2,1)S(1)}, u32[]{:S(2)}, u32[]{:S(2)}) collective-permute-start(bf16[2,6,1152]{2,1,0:T(8,128)(2,1)S(1)} %fusion.40), channel_id=1, source_target_pairs={{0,1},{1,2},{2,3},{3,4},{4,5},{5,6},{6,7},{7,8},{8,9},{9,10},{10,1... | collective-permute-start | bytes 82952 | tf_op jit(solution)/shard_map/ppermute | solution.py:24
  21.0 0.6 copy-start.7
  21.6 7.6 %collective-permute-start.1 = (bf16[2,6,1152]{2,1,0:T(8,128)(2,1)S(1)}, bf16[2,6,1152]{2,1,0:T(8,128)(2,1)S(1)}, u32[]{:S(2)}, u32[]{:S(2)}) collective-permute-start(bf16[2,6,1152]{2,1,0:T(8,128)(2,1)S(1)} %collective-permute-done), channel_id=1, source_target_pairs={{0,1},{1,2},{2,3},{3,4},{4,5},{5,6},{6,7},{7,8},{8,9},{9,10},{10,1... | collective-permute-start | bytes 82952 | tf_op jit(solution)/shard_map/ppermute | solution.py:24
  29.2 0.6 copy-start.8
  29.8 7.6 %collective-permute-start.2 = (bf16[2,6,1152]{2,1,0:T(8,128)(2,1)S(1)}, bf16[2,6,1152]{2,1,0:T(8,128)(2,1)S(1)}, u32[]{:S(2)}, u32[]{:S(2)}) collective-permute-start(bf16[2,6,1152]{2,1,0:T(8,128)(2,1)S(1)} %collective-permute-done.1), channel_id=1, source_target_pairs={{0,1},{1,2},{2,3},{3,4},{4,5},{5,6},{6,7},{7,8},{8,9},{9,10},{10,1... | collective-permute-start | bytes 82952 | tf_op jit(solution)/shard_map/ppermute | solution.py:24
  37.3 0.6 copy-start.9
  38.0 7.6 %collective-permute-start.3 = (bf16[2,6,1152]{2,1,0:T(8,128)(2,1)S(1)}, bf16[2,6,1152]{2,1,0:T(8,128)(2,1)S(1)}, u32[]{:S(2)}, u32[]{:S(2)}) collective-permute-start(bf16[2,6,1152]{2,1,0:T(8,128)(2,1)S(1)} %collective-permute-done.2), channel_id=1, source_target_pairs={{0,1},{1,2},{2,3},{3,4},{4,5},{5,6},{6,7},{7,8},{8,9},{9,10},{10,1... | collective-permute-start | bytes 82952 | tf_op jit(solution)/shard_map/ppermute | solution.py:24
  45.5 0.6 copy-start.10
  46.1 7.6 %collective-permute-start.4 = (bf16[2,6,1152]{2,1,0:T(8,128)(2,1)S(1)}, bf16[2,6,1152]{2,1,0:T(8,128)(2,1)S(1)}, u32[]{:S(2)}, u32[]{:S(2)}) collective-permute-start(bf16[2,6,1152]{2,1,0:T(8,128)(2,1)S(1)} %collective-permute-done.3), channel_id=1, source_target_pairs={{0,1},{1,2},{2,3},{3,4},{4,5},{5,6},{6,7},{7,8},{8,9},{9,10},{10,1... | collective-permute-start | bytes 82952 | tf_op jit(solution)/shard_map/ppermute | solution.py:24
  53.7 0.6 copy-start.11
  54.3 7.6 %collective-permute-start.5 = (bf16[2,6,1152]{2,1,0:T(8,128)(2,1)S(1)}, bf16[2,6,1152]{2,1,0:T(8,128)(2,1)S(1)}, u32[]{:S(2)}, u32[]{:S(2)}) collective-permute-start(bf16[2,6,1152]{2,1,0:T(8,128)(2,1)S(1)} %collective-permute-done.4), channel_id=1, source_target_pairs={{0,1},{1,2},{2,3},{3,4},{4,5},{5,6},{6,7},{7,8},{8,9},{9,10},{10,1... | collective-permute-start | bytes 82952 | tf_op jit(solution)/shard_map/ppermute | solution.py:24
  61.8 0.6 copy-start.12
  62.5 7.6 %collective-permute-start.6 = (bf16[2,6,1152]{2,1,0:T(8,128)(2,1)S(1)}, bf16[2,6,1152]{2,1,0:T(8,128)(2,1)S(1)}, u32[]{:S(2)}, u32[]{:S(2)}) collective-permute-start(bf16[2,6,1152]{2,1,0:T(8,128)(2,1)S(1)} %collective-permute-done.5), channel_id=1, source_target_pairs={{0,1},{1,2},{2,3},{3,4},{4,5},{5,6},{6,7},{7,8},{8,9},{9,10},{10,1... | collective-permute-start | bytes 82952 | tf_op jit(solution)/shard_map/ppermute | solution.py:24
  70.0 0.6 copy-start.13
  70.6 7.6 %collective-permute-start.7 = (bf16[2,6,1152]{2,1,0:T(8,128)(2,1)S(1)}, bf16[2,6,1152]{2,1,0:T(8,128)(2,1)S(1)}, u32[]{:S(2)}, u32[]{:S(2)}) collective-permute-start(bf16[2,6,1152]{2,1,0:T(8,128)(2,1)S(1)} %collective-permute-done.6), channel_id=1, source_target_pairs={{0,1},{1,2},{2,3},{3,4},{4,5},{5,6},{6,7},{7,8},{8,9},{9,10},{10,1... | collective-permute-start | bytes 82952 | tf_op jit(solution)/shard_map/ppermute | solution.py:24
  78.2 0.6 copy-start.14
  78.8 7.6 %collective-permute-start.8 = (bf16[2,6,1152]{2,1,0:T(8,128)(2,1)S(1)}, bf16[2,6,1152]{2,1,0:T(8,128)(2,1)S(1)}, u32[]{:S(2)}, u32[]{:S(2)}) collective-permute-start(bf16[2,6,1152]{2,1,0:T(8,128)(2,1)S(1)} %collective-permute-done.7), channel_id=1, source_target_pairs={{0,1},{1,2},{2,3},{3,4},{4,5},{5,6},{6,7},{7,8},{8,9},{9,10},{10,1... | collective-permute-start | bytes 82952 | tf_op jit(solution)/shard_map/ppermute | solution.py:24
  86.3 0.6 copy-start.15
  87.0 7.6 %collective-permute-start.9 = (bf16[2,6,1152]{2,1,0:T(8,128)(2,1)S(1)}, bf16[2,6,1152]{2,1,0:T(8,128)(2,1)S(1)}, u32[]{:S(2)}, u32[]{:S(2)}) collective-permute-start(bf16[2,6,1152]{2,1,0:T(8,128)(2,1)S(1)} %collective-permute-done.8), channel_id=1, source_target_pairs={{0,1},{1,2},{2,3},{3,4},{4,5},{5,6},{6,7},{7,8},{8,9},{9,10},{10,1... | collective-permute-start | bytes 82952 | tf_op jit(solution)/shard_map/ppermute | solution.py:24
  94.5 0.6 copy-start.16
  95.1 7.6 %collective-permute-start.10 = (bf16[2,6,1152]{2,1,0:T(8,128)(2,1)S(1)}, bf16[2,6,1152]{2,1,0:T(8,128)(2,1)S(1)}, u32[]{:S(2)}, u32[]{:S(2)}) collective-permute-start(bf16[2,6,1152]{2,1,0:T(8,128)(2,1)S(1)} %collective-permute-done.9), channel_id=1, source_target_pairs={{0,1},{1,2},{2,3},{3,4},{4,5},{5,6},{6,7},{7,8},{8,9},{9,10},{10,1... | collective-permute-start | bytes 82952 | tf_op jit(solution)/shard_map/ppermute | solution.py:24
  102.7 0.6 copy-start.17
  103.3 7.6 %collective-permute-start.11 = (bf16[2,6,1152]{2,1,0:T(8,128)(2,1)S(1)}, bf16[2,6,1152]{2,1,0:T(8,128)(2,1)S(1)}, u32[]{:S(2)}, u32[]{:S(2)}) collective-permute-start(bf16[2,6,1152]{2,1,0:T(8,128)(2,1)S(1)} %collective-permute-done.10), channel_id=1, source_target_pairs={{0,1},{1,2},{2,3},{3,4},{4,5},{5,6},{6,7},{7,8},{8,9},{9,10},{10,1... | collective-permute-start | bytes 82952 | tf_op jit(solution)/shard_map/ppermute | solution.py:24
  110.8 0.6 copy-start.18
  111.4 7.6 %collective-permute-start.12 = (bf16[2,6,1152]{2,1,0:T(8,128)(2,1)S(1)}, bf16[2,6,1152]{2,1,0:T(8,128)(2,1)S(1)}, u32[]{:S(2)}, u32[]{:S(2)}) collective-permute-start(bf16[2,6,1152]{2,1,0:T(8,128)(2,1)S(1)} %collective-permute-done.11), channel_id=1, source_target_pairs={{0,1},{1,2},{2,3},{3,4},{4,5},{5,6},{6,7},{7,8},{8,9},{9,10},{10,1... | collective-permute-start | bytes 82952 | tf_op jit(solution)/shard_map/ppermute | solution.py:24
  119.0 0.6 copy-start.19
  119.6 7.6 %collective-permute-start.13 = (bf16[2,6,1152]{2,1,0:T(8,128)(2,1)S(1)}, bf16[2,6,1152]{2,1,0:T(8,128)(2,1)S(1)}, u32[]{:S(2)}, u32[]{:S(2)}) collective-permute-start(bf16[2,6,1152]{2,1,0:T(8,128)(2,1)S(1)} %collective-permute-done.12), channel_id=1, source_target_pairs={{0,1},{1,2},{2,3},{3,4},{4,5},{5,6},{6,7},{7,8},{8,9},{9,10},{10,1... | collective-permute-start | bytes 82952 | tf_op jit(solution)/shard_map/ppermute | solution.py:24
  127.2 0.6 copy-start.20
  127.2 7.7 %collective-permute-start.14 = (bf16[2,6,1152]{2,1,0:T(8,128)(2,1)S(1)}, bf16[2,6,1152]{2,1,0:T(8,128)(2,1)}, u32[]{:S(2)}, u32[]{:S(2)}) collective-permute-start(bf16[2,6,1152]{2,1,0:T(8,128)(2,1)S(1)} %collective-permute-done.13), channel_id=1, source_target_pairs={{0,1},{1,2},{2,3},{3,4},{4,5},{5,6},{6,7},{7,8},{8,9},{9,10},{10,1... | collective-permute-start | bytes 82952 | tf_op jit(solution)/shard_map/ppermute | solution.py:24
  162.2 15.3 %copy-start.3 = (bf16[2,192,1152]{2,1,0:T(8,128)(2,1)}, bf16[2,192,1152]{2,1,0:T(8,128)(2,1)S(1)}, u32[]{:S(2)}) copy-start(bf16[2,192,1152]{2,1,0:T(8,128)(2,1)S(1)} %concatenate.15) | copy-start | bytes 2654212
  169.4 38.6 %all-reduce.7.cloned.1.call-start = ((), (), s32[]{:S(2)}) async-start(), calls=%async_computation | async-start | bytes 3145728 | tf_op jit(solution)/shard_map/psum | solution.py:38
  177.5 181.5 %all-reduce.9.cloned.1.call-start = ((), (), s32[]{:S(2)}) async-start(), calls=%async_computation.1 | async-start | bytes 1572864 | tf_op jit(solution)/shard_map/psum | solution.py:73
  188.9 19.1 %copy-start.6 = (f32[2,2048]{1,0:T(2,128)S(1)}, f32[2,2048]{1,0:T(2,128)}, u32[]{:S(2)}) copy-start(f32[2,2048]{1,0:T(2,128)} %param.14) | copy-start | bytes 49156
  208.0 5.5 %copy-start.2 = (f32[96,2,2048]{2,0,1:T(8,128)S(1)}, f32[96,2,2048]{2,0,1:T(8,128)}, u32[]{:S(2)}) copy-start(f32[96,2,2048]{2,0,1:T(8,128)} %all-reduce.7.cloned.1.call-done) | copy-start | bytes 4718596
  208.0 5.7 %slice-start.2 = ((s8[4718592]{0:T(1024)(128)(4,1)}), s8[4194304]{0:T(1024)(128)(4,1)S(1)}, s32[]{:S(2)}) async-start(s8[4718592]{0:T(1024)(128)(4,1)} %bitcast.48), calls=%async_computation.5 | async-start | bytes 8388608
  209.7 4.0 %slice-start.3 = ((s8[4718592]{0:T(1024)(128)(4,1)}), s8[524288]{0:T(1024)(128)(4,1)S(1)}, s32[]{:S(2)}) async-start(s8[4718592]{0:T(1024)(128)(4,1)} %bitcast.48), calls=%async_computation.6 | async-start | bytes 1048576
  209.7 4.6 %copy-start.4 = (bf16[2048,1152]{1,0:T(8,128)(2,1)S(1)}, bf16[2048,1152]{1,0:T(8,128)(2,1)}, u32[]{:S(2)}) copy-start(bf16[2048,1152]{1,0:T(8,128)(2,1)} %get-tuple-element.6) | copy-start | bytes 14155780
  214.3 58.1 %copy-start.21 = (u32[32]{0:T(128)S(1)}, u32[32]{0:T(128)}, u32[]{:S(2)}) copy-start(u32[32]{0:T(128)} %constant.53) | copy-start | bytes 388
  265.5 8.5 %collective-permute-start.16 = (bf16[8,2304]{1,0:T(8,128)(2,1)S(1)}, bf16[8,2304]{1,0:T(8,128)(2,1)S(1)}, u32[]{:S(2)}, u32[]{:S(2)}) collective-permute-start(bf16[8,2304]{1,0:T(8,128)(2,1)S(1)} %convert.22), channel_id=1, source_target_pairs={{0,2},{1,3},{2,4},{3,5},{4,6},{5,7},{6,8},{7,9},{8,10},{9,11},{10,... | collective-permute-start | bytes 110600
  266.8 7.2 %collective-permute-start.17 = (bf16[8,2304]{1,0:T(8,128)(2,1)S(1)}, bf16[8,2304]{1,0:T(8,128)(2,1)S(1)}, u32[]{:S(2)}, u32[]{:S(2)}) collective-permute-start(bf16[8,2304]{1,0:T(8,128)(2,1)S(1)} %convert.22), channel_id=1, source_target_pairs={{0,3},{1,4},{2,5},{3,6},{4,7},{5,8},{6,9},{7,10},{8,11},{9,12},{10... | collective-permute-start | bytes 110600
  268.1 5.9 %collective-permute-start.15 = (bf16[8,2304]{1,0:T(8,128)(2,1)S(1)}, bf16[8,2304]{1,0:T(8,128)(2,1)S(1)}, u32[]{:S(2)}, u32[]{:S(2)}) collective-permute-start(bf16[8,2304]{1,0:T(8,128)(2,1)S(1)} %convert.22), channel_id=1, source_target_pairs={{0,1},{1,2},{2,3},{3,4},{4,5},{5,6},{6,7},{7,8},{8,9},{9,10},{10,1... | collective-permute-start | bytes 110600
  270.0 4.0 %collective-permute-start.18 = (bf16[6,2304]{1,0:T(8,128)(2,1)S(1)}, bf16[6,2304]{1,0:T(8,128)(2,1)S(1)}, u32[]{:S(2)}, u32[]{:S(2)}) collective-permute-start(bf16[6,2304]{1,0:T(8,128)(2,1)S(1)} %slice.36), channel_id=1, source_target_pairs={{0,4},{1,5},{2,6},{3,7},{4,8},{5,9},{6,10},{7,11},{8,12},{9,13},{1... | collective-permute-start | bytes 82952
  327.4 10.9 %slice-start = ((s8[4718592]{0:T(1024)(128)(4,1)}), s8[4194304]{0:T(1024)(128)(4,1)S(1)}, s32[]{:S(2)}) async-start(s8[4718592]{0:T(1024)(128)(4,1)} %bitcast.46), calls=%async_computation.3 | async-start | bytes 8388608
  327.4 10.9 %slice-start.4 = ((s8[4718592]{0:T(1024)(128)(4,1)}), s8[4194304]{0:T(1024)(128)(4,1)S(1)}, s32[]{:S(2)}) async-start(s8[4718592]{0:T(1024)(128)(4,1)} %bitcast.50), calls=%async_computation.7 | async-start | bytes 8388608
  333.1 5.1 %slice-start.1 = ((s8[4718592]{0:T(1024)(128)(4,1)}), s8[524288]{0:T(1024)(128)(4,1)S(1)}, s32[]{:S(2)}) async-start(s8[4718592]{0:T(1024)(128)(4,1)} %bitcast.46), calls=%async_computation.4 | async-start | bytes 1048576
  333.1 5.1 %slice-start.5 = ((s8[4718592]{0:T(1024)(128)(4,1)}), s8[524288]{0:T(1024)(128)(4,1)S(1)}, s32[]{:S(2)}) async-start(s8[4718592]{0:T(1024)(128)(4,1)} %bitcast.50), calls=%async_computation.8 | async-start | bytes 1048576
  359.1 10.5 %copy-start.1 = (bf16[2,576,1152]{2,1,0:T(8,128)(2,1)S(1)}, bf16[2,576,1152]{2,1,0:T(8,128)(2,1)}, u32[]{:S(2)}) copy-start(bf16[2,576,1152]{2,1,0:T(8,128)(2,1)} %param.12) | copy-start | bytes 7962628
Sparse Core Ops, SparseCore 0:
  169.5 14.4 all-reduce.10
  186.4 21.5 all-reduce.6
  342.5 14.8 all-reduce.8
